TPU v7x, 32 devices: a whole 2x2x4 slice. The times are simulated.
32 devices in a mesh: rep: 8 (over y, x, core), fsdp: 4 (over z).
Axes of the slice: x: 2, y: 2, z: 4, core: 2. Of those that a mesh axis runs over, the one named last changes fastest.
Arguments:
- tokens: bfloat16 [8192, 1024], P(('rep', 'fsdp')), may hold values from -6 to 6
- doc_lengths: int32 [32, 8], P(('rep', 'fsdp')), may hold values from 0 to 256, as said below
- attn_norm: bfloat16 [1024], P('fsdp'), may hold values from 0.5 to 1.5
- w_query: bfloat16 [1024, 2048], P('fsdp'), may hold values from -0.1875 to 0.1875
- key_matrix: bfloat16 [1024, 1024], P('fsdp'), may hold values from -0.1875 to 0.1875
- value_matrix: bfloat16 [1024, 1024], P('fsdp'), may hold values from -0.1875 to 0.1875
- head_norms: bfloat16 [2, 128], replicated, may hold values from 0.25 to 1.75
- w_out: bfloat16 [2048, 1024], P('fsdp'), may hold values from -0.5 to 0.5
- ffn_norm: bfloat16 [1024], P('fsdp'), may hold values from 0.5 to 1.5
- w_gate: bfloat16 [1024, 3072], P('fsdp'), may hold values from -0.1875 to 0.1875
- w_up: bfloat16 [1024, 3072], P('fsdp'), may hold values from -0.1875 to 0.1875
- w_down: bfloat16 [3072, 1024], P('fsdp'), may hold values from -0.109375 to 0.109375
- cotangent: bfloat16 [8192, 1024], P(('rep', 'fsdp')), may hold values from -6 to 6
Outputs:
- mixed: bfloat16 [8192, 1024], P(('rep', 'fsdp'))
- d_tokens: bfloat16 [8192, 1024], P(('rep', 'fsdp'))
- d_attn_norm: float32 [1024], P('fsdp')
- d_w_query: float32 [1024, 2048], P('fsdp')
- d_w_key: float32 [1024, 1024], P('fsdp')
- d_w_value: float32 [1024, 1024], P('fsdp')
- d_head_norms: float32 [2, 128], replicated
- d_w_out: float32 [2048, 1024], P('fsdp')
- d_ffn_norm: float32 [1024], P('fsdp')
- d_w_gate: float32 [1024, 3072], P('fsdp')
- d_w_up: float32 [1024, 3072], P('fsdp')
- d_w_down: float32 [3072, 1024], P('fsdp')
Inputs may be any that keep to these rules, and one draw needn't show every extreme that they name: `doc_lengths`: row j lists the sequences packed from the first token row of device block j onward; zeros are empty slots; each row sums to 128 or more and to 256 or less; in every draw some device holds one sequence of 256 tokens.
All inputs are finite; a program needn't handle non-finite values.
Results may differ from a plain program's by a relative error of at most 0.02.
Values may be sent and summed in bfloat16 or wider, within the bound.
A program may use at most 192 MiB of HBM per device.

v0:
```python
import math
import jax
import jax.numpy as jnp
from jax import lax
from jax.sharding import PartitionSpec as P

QUERY_HEADS = 16
KEY_VALUE_HEADS = 8
HEAD_WIDTH = 128
EPS = 1e-06
ROPE_BASE = 1000000.0
NEG_FILL = -1e30


def layout(lengths, count_of_rows):
    seq_ends = jnp.cumsum(lengths)
    seq_starts = seq_ends - lengths
    row_ids = jnp.arange(count_of_rows, dtype=jnp.int32)
    segment = jnp.sum((row_ids[:, None] >= seq_ends[None, :]).astype(jnp.int32), axis=1)
    slot_ids = jnp.arange(lengths.shape[0], dtype=jnp.int32)
    member = (segment[:, None] == slot_ids[None, :]).astype(jnp.int32)
    position = row_ids - jnp.sum(member * seq_starts[None, :], axis=1)
    live_rows = row_ids < seq_ends[-1]
    causal = (
        (segment[:, None] == segment[None, :])
        & (row_ids[None, :] <= row_ids[:, None])
        & live_rows[:, None]
    )
    allowed = causal | (row_ids[:, None] == row_ids[None, :])
    return (position, live_rows, allowed)


def rope_tables(position, width):
    half_width = width // 2
    index = jnp.arange(half_width, dtype=jnp.float32)
    freq_table = jnp.exp(index * (-2.0 * math.log(ROPE_BASE) / width))
    angle = position.astype(jnp.float32)[:, None] * freq_table[None, :]
    return (jnp.cos(angle), jnp.sin(angle))


def apply_rotation(values_in, cosine_table, sine_table):
    half_width = values_in.shape[-1] // 2
    first_half = values_in[..., :half_width]
    second_half = values_in[..., half_width:]
    cos_rows = cosine_table[:, None, :]
    sin_rows = sine_table[:, None, :]
    return jnp.concatenate(
        [
            first_half * cos_rows - second_half * sin_rows,
            second_half * cos_rows + first_half * sin_rows,
        ],
        axis=-1,
    )


def rows_product(left, right):
    return lax.dot_general(
        left, right, (((0,), (0,)), ((), ())), preferred_element_type=jnp.float32
    )


def cols_product(left, right):
    return lax.dot_general(
        left, right, (((1,), (1,)), ((), ())), preferred_element_type=jnp.float32
    )


def norm_back(grad_in, hat_rows, row_scale, gain_full):
    leading_axes = tuple(range(grad_in.ndim - 1))
    grad_gain = jnp.sum(grad_in * hat_rows, axis=leading_axes)
    scaled_grad = grad_in * gain_full
    centered = scaled_grad - hat_rows * jnp.mean(scaled_grad * hat_rows, axis=-1, keepdims=True)
    return (row_scale * centered, grad_gain)


def head_stats(values_in):
    head_scale = lax.rsqrt(jnp.mean(values_in * values_in, axis=2, keepdims=True) + EPS)
    return (values_in * head_scale, head_scale)


def per_device(
    tokens,
    doc_lengths,
    attn_norm,
    w_query,
    key_matrix,
    value_matrix,
    head_norms,
    w_out,
    ffn_norm,
    w_gate,
    w_up,
    w_down,
    cotangent,
):
    count_of_rows = tokens.shape[0]
    group_width = QUERY_HEADS // KEY_VALUE_HEADS
    score_scale = HEAD_WIDTH ** (-0.5)
    fsdp_count = lax.axis_size("fsdp")
    rep_count = lax.axis_size("rep")
    position, live_rows, allowed = layout(doc_lengths[0], count_of_rows)
    cosine_table, sine_table = rope_tables(position, HEAD_WIDTH)
    head_gains = head_norms.astype(jnp.float32)
    query_full, key_full, value_full, out_full, norm_one = (
        lax.all_gather(w_query, "fsdp", axis=0, tiled=True),
        lax.all_gather(key_matrix, "fsdp", axis=0, tiled=True),
        lax.all_gather(value_matrix, "fsdp", axis=0, tiled=True),
        lax.all_gather(w_out, "fsdp", axis=0, tiled=True),
        lax.all_gather(attn_norm, "fsdp", axis=0, tiled=True),
    )
    inputs = tokens.astype(jnp.float32)
    first_scale = lax.rsqrt(jnp.mean(inputs * inputs, axis=1, keepdims=True) + EPS)
    first_hat = inputs * first_scale
    normalized_rows = (first_hat * norm_one).astype(jnp.bfloat16)
    query = jnp.dot(normalized_rows, query_full, preferred_element_type=jnp.float32).reshape(
        count_of_rows, QUERY_HEADS, HEAD_WIDTH
    )
    keys_before_rotation = jnp.dot(
        normalized_rows, key_full, preferred_element_type=jnp.float32
    ).reshape(count_of_rows, KEY_VALUE_HEADS, HEAD_WIDTH)
    value_rows = jnp.dot(normalized_rows, value_full, preferred_element_type=jnp.float32).astype(
        jnp.bfloat16
    )
    query_hat, query_scale = head_stats(query)
    key_hat, key_scale = head_stats(keys_before_rotation)
    rotated_query = apply_rotation(query_hat * head_gains[0], cosine_table, sine_table).astype(
        jnp.bfloat16
    )
    key_rot = apply_rotation(key_hat * head_gains[1], cosine_table, sine_table).astype(jnp.bfloat16)
    query_head_rows = jnp.moveaxis(
        rotated_query.reshape(count_of_rows, KEY_VALUE_HEADS, group_width, HEAD_WIDTH), 1, 0
    )
    key_heads = jnp.moveaxis(key_rot, 1, 0)
    value_head_rows = jnp.moveaxis(
        value_rows.reshape(count_of_rows, KEY_VALUE_HEADS, HEAD_WIDTH), 1, 0
    )

    def masked_scores(query_j, key_j):
        scores = (
            jnp.einsum("tgd,sd->gts", query_j, key_j, preferred_element_type=jnp.float32)
            * score_scale
        )
        return jnp.where(allowed[None], scores, NEG_FILL)

    def attend(parts):
        query_j, key_j, value_j = parts
        scores = masked_scores(query_j, key_j)
        highest = jnp.max(scores, axis=2, keepdims=True)
        expd = jnp.exp(scores - highest)
        totals = jnp.sum(expd, axis=2, keepdims=True)
        probs = (expd / totals).astype(jnp.bfloat16)
        head_out = jnp.einsum("gts,sd->tgd", probs, value_j, preferred_element_type=jnp.float32)
        return (head_out.astype(jnp.bfloat16), (highest + jnp.log(totals))[..., 0])

    mixed_heads, lse_heads = lax.map(attend, (query_head_rows, key_heads, value_head_rows))
    attended = jnp.moveaxis(mixed_heads, 0, 1).reshape(count_of_rows, QUERY_HEADS * HEAD_WIDTH)
    hidden = inputs + jnp.dot(attended, out_full, preferred_element_type=jnp.float32)
    gate_full, up_full, down_full, norm_two = (
        lax.all_gather(w_gate, "fsdp", axis=0, tiled=True),
        lax.all_gather(w_up, "fsdp", axis=0, tiled=True),
        lax.all_gather(w_down, "fsdp", axis=0, tiled=True),
        lax.all_gather(ffn_norm, "fsdp", axis=0, tiled=True),
    )
    second_scale = lax.rsqrt(jnp.mean(hidden * hidden, axis=1, keepdims=True) + EPS)
    second_hat = hidden * second_scale
    normed_two = (second_hat * norm_two).astype(jnp.bfloat16)
    gate = jnp.dot(normed_two, gate_full, preferred_element_type=jnp.float32)
    up_part = jnp.dot(normed_two, up_full, preferred_element_type=jnp.float32)
    sigma = jax.nn.sigmoid(gate)
    activated = (gate * sigma * up_part).astype(jnp.bfloat16)
    output = hidden + jnp.dot(activated, down_full, preferred_element_type=jnp.float32)
    mixed = jnp.where(live_rows[:, None], output, 0.0).astype(jnp.bfloat16)
    gate_full, up_full, down_full, norm_two = (
        lax.all_gather(w_gate, "fsdp", axis=0, tiled=True),
        lax.all_gather(w_up, "fsdp", axis=0, tiled=True),
        lax.all_gather(w_down, "fsdp", axis=0, tiled=True),
        lax.all_gather(ffn_norm, "fsdp", axis=0, tiled=True),
    )
    d_output = jnp.where(live_rows[:, None], cotangent.astype(jnp.float32), 0.0)
    d_branch = d_output.astype(jnp.bfloat16)
    grad_down = rows_product(activated, d_branch)
    d_activated = cols_product(d_branch, down_full)
    d_gate = (d_activated * up_part * sigma * (1.0 + gate * (1.0 - sigma))).astype(jnp.bfloat16)
    d_up = (d_activated * gate * sigma).astype(jnp.bfloat16)
    grad_gate = rows_product(normed_two, d_gate)
    grad_up = rows_product(normed_two, d_up)
    d_normed_two = cols_product(d_gate, gate_full) + cols_product(d_up, up_full)
    d_hidden_norm, grad_norm_two = norm_back(d_normed_two, second_hat, second_scale, norm_two)
    d_hidden = d_output + d_hidden_norm
    ffn_shards = (
        lax.psum_scatter(
            grad_gate.astype(jnp.bfloat16), "fsdp", scatter_dimension=0, tiled=True
        ).astype(jnp.float32),
        lax.psum_scatter(
            grad_up.astype(jnp.bfloat16), "fsdp", scatter_dimension=0, tiled=True
        ).astype(jnp.float32),
        lax.psum_scatter(
            grad_down.astype(jnp.bfloat16), "fsdp", scatter_dimension=0, tiled=True
        ).astype(jnp.float32),
        lax.psum_scatter(
            grad_norm_two.astype(jnp.bfloat16), "fsdp", scatter_dimension=0, tiled=True
        ).astype(jnp.float32),
    )
    ffn_sums = (
        lax.psum(ffn_shards[0].astype(jnp.bfloat16), "rep").astype(jnp.float32),
        lax.psum(ffn_shards[1].astype(jnp.bfloat16), "rep").astype(jnp.float32),
        lax.psum(ffn_shards[2].astype(jnp.bfloat16), "rep").astype(jnp.float32),
        lax.psum(ffn_shards[3].astype(jnp.bfloat16), "rep").astype(jnp.float32),
    )
    query_full, key_full, value_full, out_full, norm_one = (
        lax.all_gather(w_query, "fsdp", axis=0, tiled=True),
        lax.all_gather(key_matrix, "fsdp", axis=0, tiled=True),
        lax.all_gather(value_matrix, "fsdp", axis=0, tiled=True),
        lax.all_gather(w_out, "fsdp", axis=0, tiled=True),
        lax.all_gather(attn_norm, "fsdp", axis=0, tiled=True),
    )
    d_attn = d_hidden.astype(jnp.bfloat16)
    grad_out = rows_product(attended, d_attn)
    attended_gradient = cols_product(d_attn, out_full).astype(jnp.bfloat16)
    head_gradients = jnp.moveaxis(
        attended_gradient.reshape(count_of_rows, KEY_VALUE_HEADS, group_width, HEAD_WIDTH), 1, 0
    )

    def attend_back(parts):
        query_j, key_j, value_j, grad_j, lse_j = parts
        scores = masked_scores(query_j, key_j)
        probs = jnp.exp(scores - lse_j[..., None])
        d_probs = jnp.einsum("tgd,sd->gts", grad_j, value_j, preferred_element_type=jnp.float32)
        center = jnp.sum(probs * d_probs, axis=2, keepdims=True)
        d_scores = (probs * (d_probs - center)).astype(jnp.bfloat16)
        d_value_j = jnp.einsum(
            "gts,tgd->sd", probs.astype(jnp.bfloat16), grad_j, preferred_element_type=jnp.float32
        )
        d_query_j = (
            jnp.einsum("gts,sd->tgd", d_scores, key_j, preferred_element_type=jnp.float32)
            * score_scale
        )
        d_key_j = (
            jnp.einsum("gts,tgd->sd", d_scores, query_j, preferred_element_type=jnp.float32)
            * score_scale
        )
        return (d_query_j, d_key_j, d_value_j)

    d_query_heads, d_key_heads, value_head_gradient = lax.map(
        attend_back, (query_head_rows, key_heads, value_head_rows, head_gradients, lse_heads)
    )
    d_query_rot = jnp.moveaxis(d_query_heads, 0, 1).reshape(count_of_rows, QUERY_HEADS, HEAD_WIDTH)
    rotated_key_gradient = jnp.moveaxis(d_key_heads, 0, 1)
    query_norm_grad = apply_rotation(d_query_rot, cosine_table, -sine_table)
    key_norm_grad = apply_rotation(rotated_key_gradient, cosine_table, -sine_table)
    query_pre_grad, grad_query_gain = norm_back(
        query_norm_grad, query_hat, query_scale, head_gains[0]
    )
    key_pre_grad, grad_key_gain = norm_back(key_norm_grad, key_hat, key_scale, head_gains[1])
    d_query = query_pre_grad.reshape(count_of_rows, QUERY_HEADS * HEAD_WIDTH).astype(jnp.bfloat16)
    key_gradient = key_pre_grad.reshape(count_of_rows, KEY_VALUE_HEADS * HEAD_WIDTH).astype(
        jnp.bfloat16
    )
    value_gradient = (
        jnp.moveaxis(value_head_gradient, 0, 1)
        .reshape(count_of_rows, KEY_VALUE_HEADS * HEAD_WIDTH)
        .astype(jnp.bfloat16)
    )
    head_norm_sums = lax.psum(jnp.stack([grad_query_gain, grad_key_gain]), ("rep", "fsdp"))
    grad_query = rows_product(normalized_rows, d_query)
    grad_key = rows_product(normalized_rows, key_gradient)
    grad_value = rows_product(normalized_rows, value_gradient)
    d_normed = (
        cols_product(d_query, query_full)
        + cols_product(key_gradient, key_full)
        + cols_product(value_gradient, value_full)
    )
    d_input_norm, grad_norm_one = norm_back(d_normed, first_hat, first_scale, norm_one)
    d_tokens = (d_hidden + d_input_norm).astype(jnp.bfloat16)
    attn_shards = (
        lax.psum_scatter(
            grad_query.astype(jnp.bfloat16), "fsdp", scatter_dimension=0, tiled=True
        ).astype(jnp.float32),
        lax.psum_scatter(
            grad_key.astype(jnp.bfloat16), "fsdp", scatter_dimension=0, tiled=True
        ).astype(jnp.float32),
        lax.psum_scatter(
            grad_value.astype(jnp.bfloat16), "fsdp", scatter_dimension=0, tiled=True
        ).astype(jnp.float32),
        lax.psum_scatter(
            grad_out.astype(jnp.bfloat16), "fsdp", scatter_dimension=0, tiled=True
        ).astype(jnp.float32),
        lax.psum_scatter(
            grad_norm_one.astype(jnp.bfloat16), "fsdp", scatter_dimension=0, tiled=True
        ).astype(jnp.float32),
    )
    attn_sums = (
        lax.psum(attn_shards[0].astype(jnp.bfloat16), "rep").astype(jnp.float32),
        lax.psum(attn_shards[1].astype(jnp.bfloat16), "rep").astype(jnp.float32),
        lax.psum(attn_shards[2].astype(jnp.bfloat16), "rep").astype(jnp.float32),
        lax.psum(attn_shards[3].astype(jnp.bfloat16), "rep").astype(jnp.float32),
        lax.psum(attn_shards[4].astype(jnp.bfloat16), "rep").astype(jnp.float32),
    )
    grad_scale = 1.0 / math.sqrt(count_of_rows * rep_count * fsdp_count)
    return (
        mixed,
        d_tokens,
        attn_sums[4] * grad_scale,
        attn_sums[0] * grad_scale,
        attn_sums[1] * grad_scale,
        attn_sums[2] * grad_scale,
        head_norm_sums * grad_scale,
        attn_sums[3] * grad_scale,
        ffn_sums[3] * grad_scale,
        ffn_sums[0] * grad_scale,
        ffn_sums[1] * grad_scale,
        ffn_sums[2] * grad_scale,
    )


def solution(mesh):
    return jax.shard_map(
        per_device,
        mesh=mesh,
        in_specs=(
            P(("rep", "fsdp"), None),
            P(("rep", "fsdp"), None),
            P("fsdp"),
            P("fsdp", None),
            P("fsdp", None),
            P("fsdp", None),
            P(),
            P("fsdp", None),
            P("fsdp"),
            P("fsdp", None),
            P("fsdp", None),
            P("fsdp", None),
            P(("rep", "fsdp"), None),
        ),
        out_specs=(
            P(("rep", "fsdp"), None),
            P(("rep", "fsdp"), None),
            P("fsdp"),
            P("fsdp", None),
            P("fsdp", None),
            P("fsdp", None),
            P(),
            P("fsdp", None),
            P("fsdp"),
            P("fsdp", None),
            P("fsdp", None),
            P("fsdp", None),
        ),
        check_vma=False,
    )
```

profile of v0, /device:TPU:0, one launch (start us, length us, event | category | flops | bytes accessed | tf_op | source)
XLA Modules:
  0.0 1459.2 jit_solution(5098814045108164669)
XLA Ops:
  12.8 12.7 all-gather
  27.7 7.8 all-gather.1
  37.2 21.1 %all-gather.12.cloned.1.call-done = bf16[1024,1024]{1,0:T(8,128)(2,1)} async-done(((bf16[256,1024]{1,0:T(8,128)(2,1)}), bf16[1024,1024]{1,0:T(8,128)(2,1)}) %all-gather.12.cloned.1.call-update) | async-done | bytes 2097168 | tf_op jit(solution)/shard_map/all_gather | solution.py:106
  58.3 2.3 fusion.95
  62.4 42.1 %all-gather.10.cloned.1.call-done = bf16[1024,1024]{1,0:T(8,128)(2,1)} async-done(((bf16[256,1024]{1,0:T(8,128)(2,1)}), bf16[1024,1024]{1,0:T(8,128)(2,1)}) %all-gather.10.cloned.1.call-update) | async-done | bytes 2097168 | tf_op jit(solution)/shard_map/all_gather | solution.py:107
  104.6 2.3 convolution_convert_fusion.9
  109.8 75.8 %all-gather.14.cloned.1.call-done = bf16[1024,2048]{1,0:T(8,128)(2,1)} async-done(((bf16[256,2048]{1,0:T(8,128)(2,1)}), bf16[1024,2048]{1,0:T(8,128)(2,1)}) %all-gather.14.cloned.1.call-update) | async-done | bytes 4194320 | tf_op jit(solution)/shard_map/all_gather | solution.py:105
  185.7 3.5 fusion.93
  195.0 35.1 %while.28 = (s32[]{:T(128)}, bf16[8,256,2,128]{1,3,2,0:T(8,128)(2,1)}, f32[8,2,256]{2,1,0:T(2,128)}, bf16[8,256,128]{1,2,0:T(8,128)(2,1)}, bf16[8,256,128]{2,1,0...) while((s32[]{:T(128)}, ...), condition=%wide.region_9.10_spmd.clone, body=%wide.region_6.9_spmd.clone.sunk | while | flops 68615680 | bytes 2117469 | solution.py:155
  230.1 36.3 %all-gather.16.cloned.1.call-done = bf16[2048,1024]{1,0:T(8,128)(2,1)} async-done(((bf16[512,1024]{1,0:T(8,128)(2,1)}), bf16[2048,1024]{1,0:T(8,128)(2,1)}) %all-gather.16.cloned.1.call-update) | async-done | bytes 4194320 | tf_op jit(solution)/shard_map/all_gather | solution.py:108
  266.4 3.9 multiply_reduce_fusion.6
  271.4 110.3 %all-gather.18.cloned.1.call-done = bf16[1024,3072]{1,0:T(8,128)(2,1)} async-done(((bf16[256,3072]{1,0:T(8,128)(2,1)}), bf16[1024,3072]{1,0:T(8,128)(2,1)}) %all-gather.18.cloned.1.call-update) | async-done | bytes 6291472 | tf_op jit(solution)/shard_map/all_gather | solution.py:159
  381.7 6.2 fusion.100
  388.0 108.8 %all-gather.20.cloned.1.call-done = bf16[1024,3072]{1,0:T(8,128)(2,1)} async-done(((bf16[256,3072]{1,0:T(8,128)(2,1)}), bf16[1024,3072]{1,0:T(8,128)(2,1)}) %all-gather.20.cloned.1.call-update) | async-done | bytes 6291472 | tf_op jit(solution)/shard_map/all_gather | solution.py:160
  496.8 6.2 fusion.101
  503.0 108.9 %all-gather.22.cloned.1.call-done = bf16[3072,1024]{1,0:T(8,128)(2,1)} async-done(((bf16[768,1024]{1,0:T(8,128)(2,1)}), bf16[3072,1024]{1,0:T(8,128)(2,1)}) %all-gather.22.cloned.1.call-update) | async-done | bytes 6291472 | tf_op jit(solution)/shard_map/all_gather | solution.py:161
  612.0 8.8 multiply_convert_fusion.1
  620.8 5.8 fusion.102
  626.9 2.8 multiply_reduce_fusion.3
  631.1 2.3 convolution_convert_fusion.6
  633.4 2.8 reshape.253
  636.1 2.5 copy.171
  638.6 74.3 %while.29 = (s32[]{:T(128)}, f32[8,256,2,128]{1,3,2,0:T(8,128)}, f32[8,256,128]{2,1,0:T(8,128)}, bf16[8,256,128]{1,2,0:T(8,128)(2,1)}, bf16[8,256,128]{2,1,0:T(8...) while((s32[]{:T(128)}, f32[8,256,2,128]{1,3,2,0:T(8,128)}, ...), condition=%wide.region_14.15_spmd.clone, body=%wide.region_12.14_spmd.clone.sunk | while | flops 169442816 | bytes 5325177 | solution.py:244
  644.3 1.8 fusion.175
  646.1 1.8 fusion.176
  653.6 1.8 fusion.175
  655.4 1.8 fusion.176
  662.9 1.8 fusion.175
  664.7 1.8 fusion.176
  672.2 1.8 fusion.175
  674.0 1.8 fusion.176
  681.5 1.8 fusion.175
  690.7 1.8 fusion.175
  700.0 1.8 fusion.175
  709.3 1.8 fusion.175
  712.9 2.0 multiply_subtract_fusion.1
  722.0 2.2 convolution_convert_fusion.8
  724.3 3.2 convolution_convert_fusion.7
  728.2 3.2 fusion.99
  731.4 3.7 copy.126
  735.1 3.7 copy.127
  738.8 2.7 multiply_subtract_fusion
  741.5 2.3 multiply_reduce_fusion.1
  745.4 3.3 fusion.59
  748.7 3.4 convolution_convert_fusion.5
  753.3 4.5 convolution_convert_fusion.4
  757.9 5.9 convolution_convert_fusion.3
  763.9 5.9 convolution_convert_fusion.2
  770.8 5.9 convolution_convert_fusion.1
  776.8 35.9 %reduce-scatter.12.cloned.1.call-done = bf16[256,1024]{1,0:T(8,128)(2,1)} async-done(((bf16[1024,1024]{1,0:T(8,128)(2,1)}), bf16[256,1024]{1,0:T(8,128)(2,1)}) %reduce-scatter.12.cloned.1.call-update) | async-done | bytes 524304 | tf_op jit(solution)/shard_map/reduce_scatter | solution.py:282
  812.7 78.3 %reduce-scatter.8.cloned.1.call-done = bf16[256,2048]{1,0:T(8,128)(2,1)} async-done(((bf16[1024,2048]{1,0:T(8,128)(2,1)}), bf16[256,2048]{1,0:T(8,128)(2,1)}) %reduce-scatter.8.cloned.1.call-update) | async-done | bytes 1048592 | tf_op jit(solution)/shard_map/reduce_scatter | solution.py:276
  890.9 79.7 %reduce-scatter.14.cloned.1.call-done = bf16[512,1024]{1,0:T(8,128)(2,1)} async-done(((bf16[2048,1024]{1,0:T(8,128)(2,1)}), bf16[512,1024]{1,0:T(8,128)(2,1)}) %reduce-scatter.14.cloned.1.call-update) | async-done | bytes 1048592 | tf_op jit(solution)/shard_map/reduce_scatter | solution.py:285
  970.6 113.4 %reduce-scatter.16.cloned.1.call-done = bf16[256,3072]{1,0:T(8,128)(2,1)} async-done(((bf16[1024,3072]{1,0:T(8,128)(2,1)}), bf16[256,3072]{1,0:T(8,128)(2,1)}) %reduce-scatter.16.cloned.1.call-update) | async-done | bytes 1572880 | tf_op jit(solution)/shard_map/reduce_scatter | solution.py:191
  1084.1 113.6 %reduce-scatter.18.cloned.1.call-done = bf16[256,3072]{1,0:T(8,128)(2,1)} async-done(((bf16[1024,3072]{1,0:T(8,128)(2,1)}), bf16[256,3072]{1,0:T(8,128)(2,1)}) %reduce-scatter.18.cloned.1.call-update) | async-done | bytes 1572880 | tf_op jit(solution)/shard_map/reduce_scatter | solution.py:194
  1197.7 113.5 %reduce-scatter.20.cloned.1.call-done = bf16[768,1024]{1,0:T(8,128)(2,1)} async-done(((bf16[3072,1024]{1,0:T(8,128)(2,1)}), bf16[768,1024]{1,0:T(8,128)(2,1)}) %reduce-scatter.20.cloned.1.call-update) | async-done | bytes 1572880 | tf_op jit(solution)/shard_map/reduce_scatter | solution.py:197
  1313.1 3.6 fusion.103
  1318.3 2.1 fusion.72
  1320.4 10.9 all-reduce.4
  1331.5 12.9 all-reduce.2
  1344.5 38.4 %psum.74 = f32[2,128]{1,0:T(2,128)S(1)} all-reduce(f32[2,128]{1,0:T(2,128)S(1)} %pad_maximum_fusion.2), channel_id=1, replica_groups=mesh['rep'=8,'fsdp'=4] {'rep','fsdp'}, use_global_device_ids=true, to_apply=%region_31.32 | all-reduce | flops 256 | bytes 2048 | tf_op jit(solution)/shard_map/psum | solution.py:264
  1385.1 5.7 fusion.65
  1390.8 48.7 %all-reduce.7.cloned.1.call-done = (bf16[256,2048]{1,0:T(8,128)(2,1)}, bf16[256,1024]{1,0:T(8,128)(2,1)}, bf16[256,1024]{1,0:T(8,128)(2,1)}, bf16[512,1024]{1,0:...) async-done(((bf16[256,2048]{1,0:T(8,128)(2,1)}, bf16[256,1024]{1,0:T(8,128)(2,1)}, bf16[256,1024]{1,0:T(8,128)(2,1)}, ...) | async-done | bytes 7864336 | tf_op jit(solution)/shard_map/psum | solution.py:293
  1439.5 3.6 convert_multiply_fusion
  1447.4 3.5 convert_multiply_fusion.1
  (297 shorter events, 133.0 us)
Async XLA Ops:
  7.2 51.1 %all-gather.12.cloned.1.call-start = ((), (), s32[]{:S(2)}) async-start(), calls=%async_computation.8 | async-start | bytes 2621440 | tf_op jit(solution)/shard_map/all_gather | solution.py:106
  7.9 96.7 %all-gather.10.cloned.1.call-start = ((), (), s32[]{:S(2)}) async-start(), calls=%async_computation.7 | async-start | bytes 2621440 | tf_op jit(solution)/shard_map/all_gather | solution.py:107
  8.7 177.0 %all-gather.14.cloned.1.call-start = ((), (), s32[]{:S(2)}) async-start(), calls=%async_computation.9 | async-start | bytes 5242880 | tf_op jit(solution)/shard_map/all_gather | solution.py:105
  9.4 257.0 %all-gather.16.cloned.1.call-start = ((), (), s32[]{:S(2)}) async-start(), calls=%async_computation.10 | async-start | bytes 5242880 | tf_op jit(solution)/shard_map/all_gather | solution.py:108
  10.0 2.0 copy-start.47
  10.0 2.8 copy-start.48
  10.0 15.5 %copy-start = (bf16[256,1024]{1,0:T(8,128)(2,1)S(1)}, bf16[256,1024]{1,0:T(8,128)(2,1)}, u32[]{:S(2)}) copy-start(bf16[256,1024]{1,0:T(8,128)(2,1)} %param.17) | copy-start | bytes 1572868
  10.0 371.7 %all-gather.18.cloned.1.call-start = ((), (), s32[]{:S(2)}) async-start(), calls=%async_computation.11 | async-start | bytes 7864320 | tf_op jit(solution)/shard_map/all_gather | solution.py:159
  10.6 15.1 %copy-start.49 = (bf16[2,128]{1,0:T(2,128)(2,1)S(1)}, bf16[2,128]{1,0:T(2,128)(2,1)}, u32[]{:S(2)}) copy-start(bf16[2,128]{1,0:T(2,128)(2,1)} %param.23) | copy-start | bytes 1540
  10.6 17.1 %copy-start.50 = (bf16[256]{0:T(256)(128)(2,1)S(1)}, bf16[256]{0:T(256)(128)(2,1)}, u32[]{:S(2)}) copy-start(bf16[256]{0:T(256)(128)(2,1)} %param.25) | copy-start | bytes 1540
  10.6 486.2 %all-gather.20.cloned.1.call-start = ((), (), s32[]{:S(2)}) async-start(), calls=%async_computation.12 | async-start | bytes 7864320 | tf_op jit(solution)/shard_map/all_gather | solution.py:160
  11.2 600.8 %all-gather.22.cloned.1.call-start = ((), (), s32[]{:S(2)}) async-start(), calls=%async_computation.13 | async-start | bytes 7864320 | tf_op jit(solution)/shard_map/all_gather | solution.py:161
  11.9 764.9 %reduce-scatter.10.cloned.1.call-start = ((), (), s32[]{:S(2)}) async-start(), calls=%async_computation.15 | async-start | bytes 2621440 | tf_op jit(solution)/shard_map/reduce_scatter | solution.py:279
  25.7 78.8 %copy-start.30 = (f32[256]{0:T(256)}, f32[256]{0:T(256)S(1)}, u32[]{:S(2)}) copy-start(f32[256]{0:T(256)S(1)} %add_rsqrt_fusion.3) | copy-start | bytes 3076
  26.3 35.0 %copy-start.42 = (f32[128]{0:T(128)}, f32[128]{0:T(128)S(1)}, u32[]{:S(2)}) copy-start(f32[128]{0:T(128)S(1)} %get-tuple-element.285) | copy-start | bytes 1540
  37.2 71.9 %copy-start.24 = (f32[256,64]{1,0:T(8,128)}, f32[256,64]{1,0:T(8,128)S(1)}, u32[]{:S(2)}) copy-start(f32[256,64]{1,0:T(8,128)S(1)} %get-tuple-element.282) | copy-start | bytes 196612
  60.6 1.0 copy-start.1
  189.2 1.3 copy-start.7
  191.2 0.9 copy-start.25
  230.1 40.2 %copy-start.11 = (bf16[8,256,128]{2,1,0:T(8,128)(2,1)}, bf16[8,256,128]{2,1,0:T(8,128)(2,1)S(1)}, u32[]{:S(2)}) copy-start(bf16[8,256,128]{2,1,0:T(8,128)(2,1)S(1)} %get-tuple-element.527) | copy-start | bytes 1572868
  266.4 4.9 copy-start.34
  270.3 1.0 copy-start.13
  270.3 1.0 copy-start.38
  620.8 5.8 copy-start.21
  620.8 5.8 copy-start.20
  620.8 5.8 copy-start.14
  620.8 5.8 copy-start.35
  620.8 5.8 copy-start.39
  620.8 6.0 copy-start.45
  626.9 2.8 copy-start.18
  626.9 2.8 copy-start.32
  626.9 4.2 copy-start.46
  630.1 1.0 copy-start.4
  712.9 2.0 copy-start.2
  712.9 2.0 copy-start.43
  716.5 3.4 copy-start.36
  717.3 2.6 copy-start.3
  717.3 2.6 copy-start.12
  720.0 2.1 copy-start.31
  724.2 88.5 %reduce-scatter.12.cloned.1.call-start = ((), (), s32[]{:S(2)}) async-start(), calls=%async_computation.16 | async-start | bytes 2621440 | tf_op jit(solution)/shard_map/reduce_scatter | solution.py:282
  727.5 163.4 %reduce-scatter.8.cloned.1.call-start = ((), (), s32[]{:S(2)}) async-start(), calls=%async_computation.14 | async-start | bytes 5242880 | tf_op jit(solution)/shard_map/reduce_scatter | solution.py:276
  738.8 2.7 copy-start.41
  743.8 1.6 copy-start.8
  752.1 1.2 copy-start.5
  752.1 218.5 %reduce-scatter.14.cloned.1.call-start = ((), (), s32[]{:S(2)}) async-start(), calls=%async_computation.17 | async-start | bytes 5242880 | tf_op jit(solution)/shard_map/reduce_scatter | solution.py:285
  757.9 326.2 %reduce-scatter.16.cloned.1.call-start = ((), (), s32[]{:S(2)}) async-start(), calls=%async_computation.18 | async-start | bytes 7864320 | tf_op jit(solution)/shard_map/reduce_scatter | solution.py:191
  763.8 433.9 %reduce-scatter.18.cloned.1.call-start = ((), (), s32[]{:S(2)}) async-start(), calls=%async_computation.19 | async-start | bytes 7864320 | tf_op jit(solution)/shard_map/reduce_scatter | solution.py:194
  769.7 1.0 copy-start.19
  769.7 1.0 copy-start.33
  769.8 541.4 %reduce-scatter.20.cloned.1.call-start = ((), (), s32[]{:S(2)}) async-start(), calls=%async_computation.20 | async-start | bytes 7864320 | tf_op jit(solution)/shard_map/reduce_scatter | solution.py:197
  776.7 662.8 %all-reduce.7.cloned.1.call-start = ((), (), s32[]{:S(2)}) async-start(), calls=%async_computation.21 | async-start | bytes 15728640 | tf_op jit(solution)/shard_map/psum | solution.py:293
  1313.1 3.6 copy-start.6
  1313.1 3.6 copy-start.10
  1316.7 1.6 copy-start.17
  1318.3 2.1 copy-start.44
  1318.3 26.1 %copy-start.37 = (f32[1024]{0:T(1024)S(1)}, f32[1024]{0:T(1024)}, u32[]{:S(2)}) copy-start(f32[1024]{0:T(1024)} %get-tuple-element.269) | copy-start | bytes 12292
  1382.8 2.2 copy-start.15
  1382.8 2.2 copy-start.16
  1439.5 3.6 copy-start.27
  1443.1 1.6 copy-start.26
  1444.7 1.9 copy-start.22
  1444.7 2.6 copy-start.23
  1447.4 3.6 copy-start.28
  1447.4 3.6 copy-start.29
  (3 other events, 2.1 us)
Sparse Core Ops, SparseCore 0:
  9.6 48.6 all-gather.11
  59.9 44.6 all-gather.9
  106.1 79.4 all-gather.13
  187.1 79.2 all-gather.15
  267.8 113.8 all-gather.17
  383.2 113.5 all-gather.19
  498.4 113.5 all-gather.21
  724.3 42.1 reduce-scatter.9
  769.5 43.1 reduce-scatter.11
  814.8 76.0 reduce-scatter.7
  893.3 77.2 reduce-scatter.13
  972.8 111.2 reduce-scatter.15
  1086.4 111.2 reduce-scatter.17
  1199.9 111.2 reduce-scatter.19
  1315.2 124.2 all-reduce.6
where the time goes:
time: 1470 us; the launch traced here: 1460 us
  waiting for transfers between devices  1090 us (74%)
  matrix products  172 us (12%)
  blocking collectives  82.7 us (6%)
  other arithmetic  54.4 us (4%)
  local copies, waits for them, and re-layouts  42.1 us (3%)
  between operations  15.4 us (1%)
    reduce_scatter x1, waiting for transfers between devices, per_device(): lax.psum_scatter(grad_up.astype(jnp.bfloat16), 'fsdp', scatter_dimension=...  114 us
    reduce_scatter x1, waiting for transfers between devices, per_device(): lax.psum_scatter(grad_down.astype(jnp.bfloat16), 'fsdp', scatter_dimensio...  113 us
    reduce_scatter x1, waiting for transfers between devices, per_device(): lax.psum_scatter(grad_gate.astype(jnp.bfloat16), 'fsdp', scatter_dimensio...  113 us
    all_gather x1, waiting for transfers between devices, per_device(): lax.all_gather(w_gate, 'fsdp', axis=0, tiled=True)  110 us
    all_gather x1, waiting for transfers between devices, per_device(): lax.all_gather(w_down, 'fsdp', axis=0, tiled=True)  109 us
    all_gather x1, waiting for transfers between devices, per_device(): lax.all_gather(w_up, 'fsdp', axis=0, tiled=True)  109 us
    reduce_scatter x1, waiting for transfers between devices, per_device(): lax.psum_scatter(grad_out.astype(jnp.bfloat16), 'fsdp', scatter_dimension...  79.7 us
    reduce_scatter x1, waiting for transfers between devices, per_device(): lax.psum_scatter(grad_query.astype(jnp.bfloat16), 'fsdp', scatter_dimensi...  78.3 us
  transfers between devices with their start and end apart: 15, of which 14 were waited for; matrix products, arithmetic and copies ran while one was open for 9% of the time, Pallas kernels for 0%

commit v1 on v0

--- a/solution.py
+++ b/solution.py
@@ -1,3 +1,4 @@
+import functools
 import math
 import jax
 import jax.numpy as jnp
@@ -10,6 +11,37 @@
 EPS = 1e-06
 ROPE_BASE = 1000000.0
 NEG_FILL = -1e30
+
+
+def shifts_all_mix(inner_x, array_dim):
+    z2, passed, e_now = (
+        jax.lax.axis_size("fsdp"),
+        jax.lax.axis_index("fsdp"),
+        inner_x.shape[array_dim],
+    )
+    runs = list(map(lambda it: (it, (it + 1) % z2), range(z2)))
+    placed = map(lambda it: (it, (it - 1) % z2), range(z2))
+    s_next = jnp.zeros(
+        (*inner_x.shape[:array_dim], z2 * e_now, *inner_x.shape[array_dim + 1 :]), inner_x.dtype
+    )
+    rack = list(placed)
+    current_block = reached = inner_x
+    val = z2 // 2
+    s_next = lax.dynamic_update_slice_in_dim(s_next, inner_x, passed * e_now, axis=array_dim)
+    for dev in range(1, val + 1):
+        current_block = jax.lax.ppermute(current_block, "fsdp", runs)
+        s_next = lax.dynamic_update_slice_in_dim(
+            s_next, current_block, (passed - dev) % z2 * e_now, axis=array_dim
+        )
+        if dev < z2 - val:
+            reached = jax.lax.ppermute(reached, "fsdp", rack)
+            s_next = lax.dynamic_update_slice_in_dim(
+                s_next, reached, (passed + dev) % z2 * e_now, axis=array_dim
+            )
+    return s_next
+
+
+watch_islands = functools.partial(shifts_all_mix, array_dim=0)
 
 
 def layout(lengths, count_of_rows):
@@ -105,7 +137,7 @@
         lax.all_gather(w_query, "fsdp", axis=0, tiled=True),
         lax.all_gather(key_matrix, "fsdp", axis=0, tiled=True),
         lax.all_gather(value_matrix, "fsdp", axis=0, tiled=True),
-        lax.all_gather(w_out, "fsdp", axis=0, tiled=True),
+        watch_islands(w_out),
         lax.all_gather(attn_norm, "fsdp", axis=0, tiled=True),
     )
     inputs = tokens.astype(jnp.float32)

time: 1470 us -> 1510 us (1.027)
  blocking collectives: 82.7 us -> 146 us
  waiting for transfers between devices: 1090 us -> 1050 us
    all_gather x1, blocking collectives: 12.7 us -> 76.1 us  [per_device(): lax.all_gather(attn_norm, 'fsdp', axis=0, tiled=True)]
    all_gather x1, waiting for transfers between devices: 110 us -> 66.5 us  [per_device(): lax.all_gather(w_gate, 'fsdp', axis=0, tiled=True)]
    ppermute x0 -> x3, waiting for transfers between devices: none -> 42.3 us  [the longest x2 42.3 us: shifts_all_mix(): current_block = jax.lax.ppermute(current_block, 'fsdp', runs)]
    all_gather x1, waiting for transfers between devices: 42.1 us -> 3.73 us  [per_device(): lax.all_gather(value_matrix, 'fsdp', axis=0, tiled=True)]
    all_gather x1, waiting for transfers between devices: 36.3 us -> 61.5 us  [per_device(): lax.all_gather(w_out, 'fsdp', axis=0, tiled=True)]
    all_gather x1, waiting for transfers between devices: 21.1 us -> 0.01 us  [per_device(): lax.all_gather(key_matrix, 'fsdp', axis=0, tiled=True)]
  transfers between devices with their start and end apart: 15 -> 18, of which waited for: 14 -> 14; matrix products, arithmetic and copies ran while one was open for 9% -> 11% of each run, Pallas kernels for 0% -> 0%
where the time goes in v1:
time: 1510 us; the launch traced here: 1500 us
  waiting for transfers between devices  1050 us (70%)
  matrix products  174 us (12%)
  blocking collectives  146 us (10%)
  other arithmetic  53.6 us (4%)
  local copies, waits for them, and re-layouts  49.6 us (3%)
  between operations  15.4 us (1%)
    reduce_scatter x1, waiting for transfers between devices, per_device(): lax.psum_scatter(grad_up.astype(jnp.bfloat16), 'fsdp', scatter_dimension=...  114 us
    reduce_scatter x1, waiting for transfers between devices, per_device(): lax.psum_scatter(grad_down.astype(jnp.bfloat16), 'fsdp', scatter_dimensio...  113 us
    reduce_scatter x1, waiting for transfers between devices, per_device(): lax.psum_scatter(grad_gate.astype(jnp.bfloat16), 'fsdp', scatter_dimensio...  113 us
    all_gather x1, waiting for transfers between devices, per_device(): lax.all_gather(w_down, 'fsdp', axis=0, tiled=True)  109 us
    all_gather x1, waiting for transfers between devices, per_device(): lax.all_gather(w_up, 'fsdp', axis=0, tiled=True)  109 us
    reduce_scatter x1, waiting for transfers between devices, per_device(): lax.psum_scatter(grad_out.astype(jnp.bfloat16), 'fsdp', scatter_dimension...  79.7 us
    reduce_scatter x1, waiting for transfers between devices, per_device(): lax.psum_scatter(grad_query.astype(jnp.bfloat16), 'fsdp', scatter_dimensi...  78.3 us
    all_gather x1, blocking collectives, per_device(): lax.all_gather(attn_norm, 'fsdp', axis=0, tiled=True)  76.1 us
  transfers between devices with their start and end apart: 18, of which 14 were waited for; matrix products, arithmetic and copies ran while one was open for 11% of the time, Pallas kernels for 0%

profile of v1, /device:TPU:0, one launch (start us, length us, event | category | flops | bytes accessed | tf_op | source)
XLA Modules:
  0.0 1501.8 jit_solution(9178255721574226169)
XLA Ops:
  11.2 3.1 collective-permute-start
  14.3 2.1 collective-permute-start.1
  16.5 2.5 broadcast_in_dim.70
  19.0 2.5 constant_dynamic-update-slice_fusion.3
  23.1 76.1 %all-gather = bf16[4,1,256]{2,1,0:T(2,128)(2,1)S(1)} all-gather(bf16[1,1,256]{2,1,0:T(2,128)(2,1)S(1)} %reshape.255), channel_id=1, replica_groups=mesh['rep'=8,'fsdp'=4] {'fsdp'}, dimensions={0}, use_global_device_ids=true | all-gather | bytes 2560 | tf_op jit(solution)/shard_map/all_gather | solution.py:141
  99.2 8.0 all-gather.1
  113.9 42.3 %collective-permute-done.2 = bf16[512,1024]{1,0:T(8,128)(2,1)S(1)} collective-permute-done((bf16[512,1024]{1,0:T(8,128)(2,1)S(1)}, bf16[512,1024]{1,0:T(8,128)(2,1)S(1)}, u32[]{:S(2)}, u32[]{:S(2)}) %collective-permute-start.2) | collective-permute-done | bytes 1048608 | tf_op jit(solution)/shard_map/ppermute | solution.py:32
  157.3 2.3 fusion.95
  161.4 3.7 all-gather.10.cloned.1.call-done
  165.2 2.3 convolution_convert_fusion.9
  170.4 75.2 %all-gather.14.cloned.1.call-done = bf16[1024,2048]{1,0:T(8,128)(2,1)} async-done(((bf16[256,2048]{1,0:T(8,128)(2,1)}), bf16[1024,2048]{1,0:T(8,128)(2,1)}) %all-gather.14.cloned.1.call-update) | async-done | bytes 4194320 | tf_op jit(solution)/shard_map/all_gather | solution.py:137
  245.7 3.5 fusion.93
  255.0 34.3 %while.28 = (s32[]{:T(128)}, bf16[8,256,2,128]{1,3,2,0:T(8,128)(2,1)}, f32[8,2,256]{2,1,0:T(2,128)}, bf16[8,256,128]{1,2,0:T(8,128)(2,1)}, bf16[8,256,128]{2,1,0...) while((s32[]{:T(128)}, ...), condition=%wide.region_9.10_spmd.clone, body=%wide.region_6.9_spmd.clone.sunk | while | flops 68615680 | bytes 2116969 | solution.py:187
  289.3 4.1 multiply_reduce_fusion.6
  294.5 66.5 %all-gather.16.cloned.1.call-done = bf16[1024,3072]{1,0:T(8,128)(2,1)} async-done(((bf16[256,3072]{1,0:T(8,128)(2,1)}), bf16[1024,3072]{1,0:T(8,128)(2,1)}) %all-gather.16.cloned.1.call-update) | async-done | bytes 6291472 | tf_op jit(solution)/shard_map/all_gather | solution.py:191
  361.0 6.2 fusion.100
  367.3 108.8 %all-gather.18.cloned.1.call-done = bf16[1024,3072]{1,0:T(8,128)(2,1)} async-done(((bf16[256,3072]{1,0:T(8,128)(2,1)}), bf16[1024,3072]{1,0:T(8,128)(2,1)}) %all-gather.18.cloned.1.call-update) | async-done | bytes 6291472 | tf_op jit(solution)/shard_map/all_gather | solution.py:192
  476.1 6.2 fusion.101
  482.3 108.8 %all-gather.20.cloned.1.call-done = bf16[3072,1024]{1,0:T(8,128)(2,1)} async-done(((bf16[768,1024]{1,0:T(8,128)(2,1)}), bf16[3072,1024]{1,0:T(8,128)(2,1)}) %all-gather.20.cloned.1.call-update) | async-done | bytes 6291472 | tf_op jit(solution)/shard_map/all_gather | solution.py:193
  591.1 8.8 multiply_convert_fusion.1
  599.9 5.8 fusion.102
  606.0 2.8 multiply_reduce_fusion.3
  610.2 61.5 %all-gather.22.cloned.1.call-done = bf16[2048,1024]{1,0:T(8,128)(2,1)} async-done(((bf16[512,1024]{1,0:T(8,128)(2,1)}), bf16[2048,1024]{1,0:T(8,128)(2,1)}) %all-gather.22.cloned.1.call-update) | async-done | bytes 4194320 | tf_op jit(solution)/shard_map/all_gather | solution.py:246
  671.7 4.8 convolution_convert_fusion.6
  676.5 2.8 reshape.253
  679.2 2.5 copy.171
  681.7 73.5 %while.29 = (s32[]{:T(128)}, f32[8,256,2,128]{1,3,2,0:T(8,128)}, f32[8,256,128]{2,1,0:T(8,128)}, bf16[8,256,128]{1,2,0:T(8,128)(2,1)}, bf16[8,256,128]{2,1,0:T(8...) while((s32[]{:T(128)}, f32[8,256,2,128]{1,3,2,0:T(8,128)}, ...), condition=%wide.region_14.15_spmd.clone, body=%wide.region_12.14_spmd.clone.sunk | while | flops 169442816 | bytes 5325185 | solution.py:276
  687.3 1.8 fusion.175
  696.5 1.8 fusion.175
  705.7 1.8 fusion.175
  714.9 1.8 fusion.175
  724.0 1.8 fusion.175
  733.2 1.8 fusion.175
  742.4 1.8 fusion.175
  751.6 1.8 fusion.175
  755.2 2.0 multiply_subtract_fusion.1
  764.3 2.2 convolution_convert_fusion.8
  766.6 3.2 convolution_convert_fusion.7
  770.5 3.3 fusion.99
  773.9 3.7 copy.127
  777.5 3.7 copy.126
  781.3 2.7 multiply_subtract_fusion
  783.9 2.3 multiply_reduce_fusion.1
  787.9 3.3 fusion.59
  791.2 3.3 convolution_convert_fusion.5
  795.7 4.5 convolution_convert_fusion.4
  800.4 5.9 convolution_convert_fusion.3
  806.3 5.9 convolution_convert_fusion.2
  813.2 5.9 convolution_convert_fusion.1
  819.3 36.0 %reduce-scatter.12.cloned.1.call-done = bf16[256,1024]{1,0:T(8,128)(2,1)} async-done(((bf16[1024,1024]{1,0:T(8,128)(2,1)}), bf16[256,1024]{1,0:T(8,128)(2,1)}) %reduce-scatter.12.cloned.1.call-update) | async-done | bytes 524304 | tf_op jit(solution)/shard_map/reduce_scatter | solution.py:314
  855.3 78.3 %reduce-scatter.8.cloned.1.call-done = bf16[256,2048]{1,0:T(8,128)(2,1)} async-done(((bf16[1024,2048]{1,0:T(8,128)(2,1)}), bf16[256,2048]{1,0:T(8,128)(2,1)}) %reduce-scatter.8.cloned.1.call-update) | async-done | bytes 1048592 | tf_op jit(solution)/shard_map/reduce_scatter | solution.py:308
  933.5 79.7 %reduce-scatter.14.cloned.1.call-done = bf16[512,1024]{1,0:T(8,128)(2,1)} async-done(((bf16[2048,1024]{1,0:T(8,128)(2,1)}), bf16[512,1024]{1,0:T(8,128)(2,1)}) %reduce-scatter.14.cloned.1.call-update) | async-done | bytes 1048592 | tf_op jit(solution)/shard_map/reduce_scatter | solution.py:317
  1013.2 113.4 %reduce-scatter.16.cloned.1.call-done = bf16[256,3072]{1,0:T(8,128)(2,1)} async-done(((bf16[1024,3072]{1,0:T(8,128)(2,1)}), bf16[256,3072]{1,0:T(8,128)(2,1)}) %reduce-scatter.16.cloned.1.call-update) | async-done | bytes 1572880 | tf_op jit(solution)/shard_map/reduce_scatter | solution.py:223
  1126.7 113.6 %reduce-scatter.18.cloned.1.call-done = bf16[256,3072]{1,0:T(8,128)(2,1)} async-done(((bf16[1024,3072]{1,0:T(8,128)(2,1)}), bf16[256,3072]{1,0:T(8,128)(2,1)}) %reduce-scatter.18.cloned.1.call-update) | async-done | bytes 1572880 | tf_op jit(solution)/shard_map/reduce_scatter | solution.py:226
  1240.3 113.5 %reduce-scatter.20.cloned.1.call-done = bf16[768,1024]{1,0:T(8,128)(2,1)} async-done(((bf16[3072,1024]{1,0:T(8,128)(2,1)}), bf16[768,1024]{1,0:T(8,128)(2,1)}) %reduce-scatter.20.cloned.1.call-update) | async-done | bytes 1572880 | tf_op jit(solution)/shard_map/reduce_scatter | solution.py:229
  1355.7 3.6 fusion.103
  1362.0 11.0 all-reduce.4
  1373.1 12.9 all-reduce.2
  1386.0 38.2 %psum.74 = f32[2,128]{1,0:T(2,128)S(1)} all-reduce(f32[2,128]{1,0:T(2,128)S(1)} %pad_maximum_fusion.2), channel_id=1, replica_groups=mesh['rep'=8,'fsdp'=4] {'rep','fsdp'}, use_global_device_ids=true, to_apply=%region_31.32 | all-reduce | flops 256 | bytes 2048 | tf_op jit(solution)/shard_map/psum | solution.py:296
  1426.5 6.0 fusion.65
  1432.5 49.7 %all-reduce.7.cloned.1.call-done = (bf16[256,2048]{1,0:T(8,128)(2,1)}, bf16[256,1024]{1,0:T(8,128)(2,1)}, bf16[256,1024]{1,0:T(8,128)(2,1)}, bf16[512,1024]{1,0:...) async-done(((bf16[256,2048]{1,0:T(8,128)(2,1)}, bf16[256,1024]{1,0:T(8,128)(2,1)}, bf16[256,1024]{1,0:T(8,128)(2,1)}, ...) | async-done | bytes 7864336 | tf_op jit(solution)/shard_map/psum | solution.py:325
  1482.1 2.9 convert_multiply_fusion.4
  1486.8 2.1 convert_multiply_fusion
  1491.6 3.5 convert_multiply_fusion.1
  (306 shorter events, 142.3 us)
Async XLA Ops:
  7.2 150.1 %all-gather.12.cloned.1.call-start = ((), (), s32[]{:S(2)}) async-start(), calls=%async_computation.8 | async-start | bytes 2621440 | tf_op jit(solution)/shard_map/all_gather | solution.py:138
  7.9 157.3 %all-gather.10.cloned.1.call-start = ((), (), s32[]{:S(2)}) async-start(), calls=%async_computation.7 | async-start | bytes 2621440 | tf_op jit(solution)/shard_map/all_gather | solution.py:139
  8.7 237.0 %all-gather.14.cloned.1.call-start = ((), (), s32[]{:S(2)}) async-start(), calls=%async_computation.9 | async-start | bytes 5242880 | tf_op jit(solution)/shard_map/all_gather | solution.py:137
  9.4 351.6 %all-gather.16.cloned.1.call-start = ((), (), s32[]{:S(2)}) async-start(), calls=%async_computation.10 | async-start | bytes 7864320 | tf_op jit(solution)/shard_map/all_gather | solution.py:191
  10.0 466.1 %all-gather.18.cloned.1.call-start = ((), (), s32[]{:S(2)}) async-start(), calls=%async_computation.11 | async-start | bytes 7864320 | tf_op jit(solution)/shard_map/all_gather | solution.py:192
  10.6 580.5 %all-gather.20.cloned.1.call-start = ((), (), s32[]{:S(2)}) async-start(), calls=%async_computation.12 | async-start | bytes 7864320 | tf_op jit(solution)/shard_map/all_gather | solution.py:193
  11.1 660.6 %all-gather.22.cloned.1.call-start = ((), (), s32[]{:S(2)}) async-start(), calls=%async_computation.13 | async-start | bytes 5242880 | tf_op jit(solution)/shard_map/all_gather | solution.py:246
  11.2 96.7 %collective-permute-start = (bf16[512,1024]{1,0:T(8,128)(2,1)}, bf16[512,1024]{1,0:T(8,128)(2,1)S(1)}, u32[]{:S(2)}, u32[]{:S(2)}) collective-permute-start(bf16[512,1024]{1,0:T(8,128)(2,1)} %param.24), channel_id=1, source_target_pairs={{0,1},{1,2},{2,3},{3,0},{4,5},{5,6},{6,7},{7,4},{8,9},{9,10},{10,1... | collective-permute-start | bytes 3145736 | tf_op jit(solution)/shard_map/ppermute | solution.py:32
  14.3 98.6 %collective-permute-start.1 = (bf16[512,1024]{1,0:T(8,128)(2,1)}, bf16[512,1024]{1,0:T(8,128)(2,1)S(1)}, u32[]{:S(2)}, u32[]{:S(2)}) collective-permute-start(bf16[512,1024]{1,0:T(8,128)(2,1)} %param.24), channel_id=1, source_target_pairs={{0,3},{1,0},{2,1},{3,2},{4,7},{5,4},{6,5},{7,6},{8,11},{9,8},{10,9... | collective-permute-start | bytes 3145736 | tf_op jit(solution)/shard_map/ppermute | solution.py:37
  16.4 802.9 %reduce-scatter.10.cloned.1.call-start = ((), (), s32[]{:S(2)}) async-start(), calls=%async_computation.15 | async-start | bytes 2621440 | tf_op jit(solution)/shard_map/reduce_scatter | solution.py:311
  19.0 2.5 copy-start.46
  19.0 2.5 copy-start.47
  19.0 2.5 copy-start.48
  19.0 3.4 copy-start
  19.0 80.2 %copy-start.49 = (bf16[256]{0:T(256)(128)(2,1)S(1)}, bf16[256]{0:T(256)(128)(2,1)}, u32[]{:S(2)}) copy-start(bf16[256]{0:T(256)(128)(2,1)} %param.25) | copy-start | bytes 1540
  22.5 142.7 %copy-start.30 = (f32[256]{0:T(256)}, f32[256]{0:T(256)S(1)}, u32[]{:S(2)}) copy-start(f32[256]{0:T(256)S(1)} %add_rsqrt_fusion.3) | copy-start | bytes 3076
  23.1 137.2 %copy-start.42 = (f32[128]{0:T(128)}, f32[128]{0:T(128)S(1)}, u32[]{:S(2)}) copy-start(f32[128]{0:T(128)S(1)} %get-tuple-element.285) | copy-start | bytes 1540
  107.9 48.3 %collective-permute-start.2 = (bf16[512,1024]{1,0:T(8,128)(2,1)S(1)}, bf16[512,1024]{1,0:T(8,128)(2,1)S(1)}, u32[]{:S(2)}, u32[]{:S(2)}) collective-permute-start(bf16[512,1024]{1,0:T(8,128)(2,1)S(1)} %collective-permute-done), channel_id=1, source_target_pairs={{0,1},{1,2},{2,3},{3,0},{4,5},{5,6},{6,7},{7,4},{8,9},{9,10},{10,1... | collective-permute-start | bytes 3145736 | tf_op jit(solution)/shard_map/ppermute | solution.py:32
  111.8 57.9 %copy-start.25 = (f32[256,64]{1,0:T(8,128)}, f32[256,64]{1,0:T(8,128)S(1)}, u32[]{:S(2)}) copy-start(f32[256,64]{1,0:T(8,128)S(1)} %get-tuple-element.282) | copy-start | bytes 196612
  159.7 1.0 copy-start.1
  249.2 1.3 copy-start.6
  289.3 4.1 copy-start.10
  289.3 5.0 copy-start.34
  293.4 1.0 copy-start.12
  599.9 5.8 copy-start.21
  599.9 5.9 copy-start.20
  599.9 5.9 copy-start.13
  599.9 5.9 copy-start.35
  599.9 5.9 copy-start.39
  599.9 6.1 copy-start.45
  606.0 2.8 copy-start.17
  606.0 2.8 copy-start.32
  755.2 2.0 copy-start.2
  755.2 2.0 copy-start.43
  758.8 3.4 copy-start.36
  759.6 2.6 copy-start.3
  759.6 2.6 copy-start.11
  762.2 2.1 copy-start.31
  766.5 88.8 %reduce-scatter.12.cloned.1.call-start = ((), (), s32[]{:S(2)}) async-start(), calls=%async_computation.16 | async-start | bytes 2621440 | tf_op jit(solution)/shard_map/reduce_scatter | solution.py:314
  769.8 163.7 %reduce-scatter.8.cloned.1.call-start = ((), (), s32[]{:S(2)}) async-start(), calls=%async_computation.14 | async-start | bytes 5242880 | tf_op jit(solution)/shard_map/reduce_scatter | solution.py:308
  781.3 2.7 copy-start.41
  786.3 1.6 copy-start.7
  794.5 1.2 copy-start.4
  794.5 218.7 %reduce-scatter.14.cloned.1.call-start = ((), (), s32[]{:S(2)}) async-start(), calls=%async_computation.17 | async-start | bytes 5242880 | tf_op jit(solution)/shard_map/reduce_scatter | solution.py:317
  800.3 326.4 %reduce-scatter.16.cloned.1.call-start = ((), (), s32[]{:S(2)}) async-start(), calls=%async_computation.18 | async-start | bytes 7864320 | tf_op jit(solution)/shard_map/reduce_scatter | solution.py:223
  806.3 434.0 %reduce-scatter.18.cloned.1.call-start = ((), (), s32[]{:S(2)}) async-start(), calls=%async_computation.19 | async-start | bytes 7864320 | tf_op jit(solution)/shard_map/reduce_scatter | solution.py:226
  812.2 1.0 copy-start.18
  812.2 1.0 copy-start.33
  812.2 541.5 %reduce-scatter.20.cloned.1.call-start = ((), (), s32[]{:S(2)}) async-start(), calls=%async_computation.20 | async-start | bytes 7864320 | tf_op jit(solution)/shard_map/reduce_scatter | solution.py:229
  819.2 662.9 %all-reduce.7.cloned.1.call-start = ((), (), s32[]{:S(2)}) async-start(), calls=%async_computation.21 | async-start | bytes 15728640 | tf_op jit(solution)/shard_map/psum | solution.py:325
  1355.6 3.6 copy-start.5
  1355.6 3.6 copy-start.9
  1359.3 1.6 copy-start.16
  1359.3 1.7 copy-start.19
  1361.0 1.0 copy-start.44
  1361.0 25.0 %copy-start.37 = (f32[1024]{0:T(1024)S(1)}, f32[1024]{0:T(1024)}, u32[]{:S(2)}) copy-start(f32[1024]{0:T(1024)} %get-tuple-element.269) | copy-start | bytes 12292
  1424.2 2.2 copy-start.14
  1424.2 2.2 copy-start.15
  1482.1 2.9 copy-start.27
  1485.0 1.8 copy-start.24
  1486.8 2.1 copy-start.28
  1486.8 2.1 copy-start.29
  1488.9 1.8 copy-start.22
  1488.9 2.6 copy-start.23
  (5 other events, 4.0 us)
Sparse Core Ops, SparseCore 0:
  9.6 81.0 all-gather.11
  92.3 72.8 all-gather.9
  166.8 78.8 all-gather.13
  247.1 113.8 all-gather.15
  362.4 113.5 all-gather.17
  477.5 113.5 all-gather.19
  592.7 78.9 all-gather.21
  766.6 42.3 reduce-scatter.9
  812.0 43.1 reduce-scatter.11
  857.4 76.0 reduce-scatter.7
  935.9 77.2 reduce-scatter.13
  1015.4 111.2 reduce-scatter.15
  1129.0 111.2 reduce-scatter.17
  1242.4 111.2 reduce-scatter.19
  1357.8 124.3 all-reduce.6
